TPU v7x, 256 devices: a whole 4x4x8 slice. The times are simulated.
256 devices in a mesh: dp: 2 (over y_hi), fsdp: 16 (over x, y_lo, core), tensor: 8 (over z).
Axes of the slice: x: 4, y: 4 (y_hi: 2, y_lo: 2; y = y_hi * 2 + y_lo), z: 8, core: 2. Of those that a mesh axis runs over, the one named last changes fastest.
Arguments:
- activations: bfloat16 [4096, 8192], P(('dp', 'fsdp'), 'tensor'), may hold values from -6 to 6
- cotangent: bfloat16 [4096, 8192], P(('dp', 'fsdp'), 'tensor'), may hold values from -6 to 6
- up_tiles: bfloat16 [1024, 128, 128], P(('fsdp', 'tensor')), may hold values from -0.1875 to 0.1875
- down_tiles: bfloat16 [1024, 128, 128], P(('fsdp', 'tensor')), may hold values from -0.125 to 0.125
- up_rows: int32 [128, 8], P(None, 'tensor'), may hold values from 0 to 63, as said below
- up_cols: int32 [128, 8], P(None, 'tensor'), may hold values from 0 to 15, as said below
- down_rows: int32 [128, 8], P(None, 'tensor'), may hold values from 0 to 15, as said below
- down_cols: int32 [128, 8], P(None, 'tensor'), may hold values from 0 to 63, as said below
Outputs:
- output: bfloat16 [4096, 8192], P(('dp', 'fsdp'), 'tensor')
- input_grad: bfloat16 [4096, 8192], P(('dp', 'fsdp'), 'tensor')
- up_grad: float32 [1024, 128, 128], P(('fsdp', 'tensor'))
- down_grad: float32 [1024, 128, 128], P(('fsdp', 'tensor'))
Inputs may be any that keep to these rules, and one draw needn't show every extreme that they name: `up_rows`: within a column, the up tiles of one hidden-unit block name distinct feature blocks. `up_cols`: every value occurs exactly 8 times in each column. `down_rows`: every value occurs exactly 8 times in each column. `down_cols`: within a column, the down tiles of one hidden-unit block name distinct feature blocks.
All inputs are finite; a program needn't handle non-finite values.
Results may differ from a plain program's by a relative error of at most 0.018.
Values may be sent and summed in bfloat16 or wider, within the bound.
No kernel may reach another device: no remote copies, remote signals or barrier semaphores. Data moves between devices by JAX's collectives and lax.ppermute only.
A program may use at most 128 MiB of HBM per device.

v0:
```python
import jax
import jax.numpy as jnp
from jax import lax
from jax.sharding import PartitionSpec as P

D = 8192
FF = 16384


inv_root_two = 0.7071067811865476
inv_root_tau = 0.3989422804014327


def gelu_parts(values):
    normal_cdf = 0.5 * (1.0 + jax.scipy.special.erf(values * inv_root_two))
    density = inv_root_tau * jnp.exp(-0.5 * values * values)
    return (values * normal_cdf, normal_cdf + values * density)


def grouped_pick(acting, far_index, hidden_blocks, block_size):
    rows_here = acting.shape[0]
    picked = acting.reshape(rows_here, -1, block_size)[:, far_index]
    return picked.reshape(rows_here, hidden_blocks, -1, block_size)


def add_far(product, far_index, model_blocks):
    rows_here = product.shape[0]
    block_size = product.shape[-1]
    flat = product.reshape(rows_here, -1, block_size)
    summed = (
        jnp.zeros((rows_here, model_blocks, block_size), jnp.float32).at[:, far_index].add(flat)
    )
    return summed.reshape(rows_here, model_blocks * block_size)


def grouped_tiles(tiles, order, hidden_blocks):
    block_size = tiles.shape[1]
    return tiles[order].reshape(hidden_blocks, -1, block_size, block_size)


def body(activations, cotangent, up_tiles, down_tiles, up_rows, up_cols, down_rows, down_cols):
    block_size = up_tiles.shape[1]
    hidden_blocks = FF // (block_size * lax.axis_size("tensor"))
    model_blocks = D // block_size
    up_order = jnp.argsort(up_cols[:, 0], stable=True)
    down_order = jnp.argsort(down_rows[:, 0], stable=True)
    up_back = jnp.argsort(up_order)
    down_back = jnp.argsort(down_order)
    up_far = up_rows[:, 0][up_order]
    down_far = down_cols[:, 0][down_order]
    full_input = lax.all_gather(activations, "tensor", axis=1, tiled=True)
    input_pick = grouped_pick(full_input, up_far, hidden_blocks, block_size)
    up_whole = lax.all_gather(up_tiles, "fsdp", axis=0, tiled=True)
    up_sorted = grouped_tiles(up_whole, up_order, hidden_blocks)
    pre_act = jnp.einsum(
        "thkb,hkbc->thc", input_pick, up_sorted, preferred_element_type=jnp.float32
    )
    gelu_out, gelu_slope = gelu_parts(pre_act)
    hidden = gelu_out.astype(jnp.bfloat16)
    down_whole = lax.all_gather(down_tiles, "fsdp", axis=0, tiled=True)
    down_sorted = grouped_tiles(down_whole, down_order, hidden_blocks)
    out_product = jnp.einsum(
        "thb,hkbc->thkc", hidden, down_sorted, preferred_element_type=jnp.float32
    )
    partial_out = add_far(out_product, down_far, model_blocks)
    output = lax.psum_scatter(
        partial_out.astype(jnp.bfloat16), "tensor", scatter_dimension=1, tiled=True
    )
    full_cotangent = lax.all_gather(cotangent, "tensor", axis=1, tiled=True)
    cot_pick = grouped_pick(full_cotangent, down_far, hidden_blocks, block_size)
    hidden_grad = jnp.einsum(
        "thkc,hkbc->thb", cot_pick, down_sorted, preferred_element_type=jnp.float32
    )
    pre_grad = (hidden_grad * gelu_slope).astype(jnp.bfloat16)
    in_product = jnp.einsum(
        "thc,hkbc->thkb", pre_grad, up_sorted, preferred_element_type=jnp.float32
    )
    partial_in = add_far(in_product, up_far, model_blocks)
    input_grad = lax.psum_scatter(
        partial_in.astype(jnp.bfloat16), "tensor", scatter_dimension=1, tiled=True
    )
    up_grouped = jnp.einsum(
        "thkb,thc->hkbc", input_pick, pre_grad, preferred_element_type=jnp.float32
    )
    down_grouped = jnp.einsum(
        "thb,thkc->hkbc", hidden, cot_pick, preferred_element_type=jnp.float32
    )
    up_rounded = up_grouped.astype(jnp.bfloat16).reshape(-1, block_size, block_size)
    down_rounded = down_grouped.astype(jnp.bfloat16).reshape(-1, block_size, block_size)
    up_term = up_rounded[up_back].astype(jnp.float32)
    down_term = down_rounded[down_back].astype(jnp.float32)
    up_part, down_part = (
        lax.psum_scatter(
            up_term.astype(jnp.bfloat16), "fsdp", scatter_dimension=0, tiled=True
        ).astype(jnp.float32),
        lax.psum_scatter(
            down_term.astype(jnp.bfloat16), "fsdp", scatter_dimension=0, tiled=True
        ).astype(jnp.float32),
    )
    up_grad, down_grad = (
        lax.psum(up_part.astype(jnp.bfloat16), "dp").astype(jnp.float32),
        lax.psum(down_part.astype(jnp.bfloat16), "dp").astype(jnp.float32),
    )
    return (output, input_grad, up_grad, down_grad)


def solution(mesh):
    in_specs = (
        P(("dp", "fsdp"), "tensor"),
        P(("dp", "fsdp"), "tensor"),
        P(("fsdp", "tensor"), None, None),
        P(("fsdp", "tensor"), None, None),
        P(None, "tensor"),
        P(None, "tensor"),
        P(None, "tensor"),
        P(None, "tensor"),
    )
    out_specs = (
        P(("dp", "fsdp"), "tensor"),
        P(("dp", "fsdp"), "tensor"),
        P(("fsdp", "tensor"), None, None),
        P(("fsdp", "tensor"), None, None),
    )
    return jax.shard_map(body, mesh=mesh, in_specs=in_specs, out_specs=out_specs, check_vma=False)
```

profile of v0, /device:TPU:8, one launch (start us, length us, event | category | flops | bytes accessed | tf_op | source)
XLA Modules:
  0.0 478.9 jit_solution(9236470539080875752)
XLA Ops:
  24.1 31.0 %all-gather.9.cloned.1.call-done = bf16[128,8192]{0,1:T(8,128)(2,1)} async-done(((bf16[128,1024]{0,1:T(8,128)(2,1)}), bf16[128,8192]{0,1:T(8,128)(2,1)}) %all-gather.9.cloned.1.call-update) | async-done | bytes 2097168 | tf_op jit(solution)/shard_map/all_gather | solution.py:51
  58.4 38.7 %all-gather.11.cloned.1.call-done = bf16[128,8192]{0,1:T(8,128)(2,1)} async-done(((bf16[128,1024]{0,1:T(8,128)(2,1)}), bf16[128,8192]{0,1:T(8,128)(2,1)}) %all-gather.11.cloned.1.call-update) | async-done | bytes 2097168 | tf_op jit(solution)/shard_map/all_gather | solution.py:69
  97.1 4.1 copy.66
  104.2 4.6 gather_fusion.5
  108.8 28.4 %all-gather.7.cloned.1.call-done = bf16[128,128,128]{2,1,0:T(8,128)(2,1)} async-done(((bf16[8,128,128]{2,1,0:T(8,128)(2,1)}), bf16[128,128,128]{2,1,0:T(8,128)(2,1)}) %all-gather.7.cloned.1.call-update) | async-done | bytes 4194320 | tf_op jit(solution)/shard_map/all_gather | solution.py:53
  137.3 5.2 %gather_fusion.2 = bf16[128,128,128]{2,1,0:T(8,128)(2,1)} fusion(bf16[128,128,128]{2,1,0:T(8,128)(2,1)} %all-gather.7.cloned.1.call-done, s32[1024]{0:T(1024)S(1)} %pad_clamp_fusion.4), kind=kCustom, calls=%fused_computation.2 | custom fusion | bytes 8389120 | tf_op jit(solution)/shard_map/gather | solution.py:38
  142.4 4.8 %convolution_bitcast_fusion.1 = f32[128,16,128]{0,2,1:T(8,128)S(1)} fusion(bf16[16,8,128,128]{3,2,1,0:T(8,128)(2,1)} %bitcast.76, bf16[128,16,8,128]{3,0,2,1:T(8,128)(2,1)} %bitcast.78), kind=kOutput, calls=%fused_computation.14 | convolution fusion | flops 536870912 | bytes 9437184 | tf_op jit(solution)/shard_map/thkb,hkbc->thc/dot_general | solution.py:55
  147.2 31.7 %all-gather.5.cloned.1.call-done = bf16[128,128,128]{2,1,0:T(8,128)(2,1)} async-done(((bf16[8,128,128]{2,1,0:T(8,128)(2,1)}), bf16[128,128,128]{2,1,0:T(8,128)(2,1)}) %all-gather.5.cloned.1.call-update) | async-done | bytes 4194320 | tf_op jit(solution)/shard_map/all_gather | solution.py:60
  179.0 5.2 %gather_fusion.1 = bf16[128,128,128]{2,1,0:T(8,128)(2,1)} fusion(bf16[128,128,128]{2,1,0:T(8,128)(2,1)} %all-gather.5.cloned.1.call-done, s32[1024]{0:T(1024)S(1)} %pad_clamp_fusion.5), kind=kCustom, calls=%fused_computation.1 | custom fusion | bytes 8389120 | tf_op jit(solution)/shard_map/gather | solution.py:38
  184.2 5.0 %fusion.2 = bf16[128,16,128,1]{0,2,3,1:T(8,128)(2,1)S(1)} fusion(bf16[16,8,128,128]{3,2,1,0:T(8,128)(2,1)} %bitcast.84, bf16[128,16,8,128]{3,0,2,1:T(8,128)(2,1)} %bitcast.86, f32[128,16,128]{0,2,1:T(8,128)S(1)} %convolution_bitcast_fusion.1), kind=kOutput, calls=%fused_computation.17 | convolution fusion | flops 539492352 | bytes 9961472 | tf_op jit(solution)/shard_map/thkc,hkbc->thb/dot_general | solution.py:71
  192.5 5.2 %gather_fusion.6 = bf16[128,128,128]{2,1,0:T(8,128)(2,1)} fusion(bf16[128,128,128]{2,1,0:T(8,128)(2,1)} %bitcast.88, s32[1024]{0:T(1024)S(1)} %pad_clamp_fusion.1), kind=kCustom, calls=%fused_computation.6 | custom fusion | bytes 8389120 | tf_op jit(solution)/shard_map/gather | solution.py:90
  200.5 5.6 %convolution_convert_fusion = bf16[16,8,128,128]{3,2,1,0:T(8,128)(2,1)} fusion(bf16[128,16,8,128]{3,0,2,1:T(8,128)(2,1)} %bitcast.87, f32[128,16,128]{0,2,1:T(8,128)S(1)} %convolution_bitcast_fusion.1), kind=kOutput, calls=%fused_computation.10 | convolution fusion | flops 540278784 | bytes 9437184 | tf_op jit(solution)/shard_map/thb,thkc->hkbc/dot_general | solution.py:85
  206.2 6.4 %copy.74 = bf16[128,128,128]{2,1,0:T(8,128)(2,1)} copy(bf16[128,128,128]{1,2,0:T(8,128)(2,1)} %bitcast.89) | data formatting | bytes 8388608 | tf_op jit(solution)/shard_map/reshape | solution.py:89
  212.5 5.3 %gather_fusion.7 = bf16[128,128,128]{2,1,0:T(8,128)(2,1)} fusion(bf16[128,128,128]{2,1,0:T(8,128)(2,1)} %copy.74, s32[1024]{0:T(1024)S(1)} %pad_clamp_fusion), kind=kCustom, calls=%fused_computation.7 | custom fusion | bytes 8389120 | tf_op jit(solution)/shard_map/gather | solution.py:91
  217.9 6.7 %fusion.13 = f32[16,8,128,128]{3,2,1,0:T(8,128)} fusion(bf16[16,8,128,128]{3,2,1,0:T(8,128)(2,1)} %bitcast.77, bf16[128,16,128,1]{0,2,3,1:T(8,128)(2,1)S(1)} %fusion.2), kind=kOutput, calls=%fused_computation.40 | convolution fusion | flops 536870912 | bytes 13107200 | tf_op jit(solution)/shard_map/thc,hkbc->thkb/dot_general | solution.py:75
  224.6 9.0 %copy.68 = f32[128,128,128]{2,0,1:T(8,128)} copy(f32[128,128,128]{0,2,1:T(8,128)} %bitcast.82) | data formatting | bytes 16777216 | tf_op jit(solution)/shard_map/reshape | solution.py:29
  236.1 26.7 %scatter_fusion.1 = f32[128,64,128]{2,0,1:T(8,128)} fusion(f32[128,64,128]{2,0,1:T(8,128)} %broadcast.42.clone.1, s32[128]{0:T(128)S(1)} %fusion.9, f32[128,128,128]{2,1,0:T(8,128)} %bitcast.81), kind=kCustom, calls=%fused_computation.9 | custom fusion | flops 2097152 | bytes 25166336 | tf_op jit(solution)/shard_map/scatter-add | solution.py:31
  268.4 6.8 %fusion.11 = f32[16,8,128,128]{3,2,1,0:T(8,128)} fusion(bf16[16,8,128,128]{3,2,1,0:T(8,128)(2,1)} %bitcast.85, f32[128,16,128]{0,2,1:T(8,128)S(1)} %convolution_bitcast_fusion.1), kind=kOutput, calls=%fused_computation.39 | convolution fusion | flops 538181632 | bytes 13631488 | tf_op jit(solution)/shard_map/thb,hkbc->thkc/dot_general | solution.py:62
  275.2 9.0 %copy.63 = f32[128,128,128]{2,0,1:T(8,128)} copy(f32[128,128,128]{0,2,1:T(8,128)} %bitcast.83) | data formatting | bytes 16777216 | tf_op jit(solution)/shard_map/reshape | solution.py:29
  286.7 26.8 %scatter_fusion = f32[128,64,128]{2,0,1:T(8,128)} fusion(f32[128,64,128]{2,0,1:T(8,128)} %broadcast.42.clone, s32[128]{0:T(128)S(1)} %fusion.8, f32[128,128,128]{2,1,0:T(8,128)} %bitcast.80), kind=kCustom, calls=%fused_computation.8 | custom fusion | flops 2097152 | bytes 25166336 | tf_op jit(solution)/shard_map/scatter-add | solution.py:31
  319.1 16.0 %reduce-scatter.11.cloned.1.call-done = bf16[8,128,128]{2,1,0:T(8,128)(2,1)} async-done(((bf16[128,128,128]{2,1,0:T(8,128)(2,1)}), bf16[8,128,128]{2,1,0:T(8,128)(2,1)}) %reduce-scatter.11.cloned.1.call-update) | async-done | bytes 262160 | tf_op jit(solution)/shard_map/reduce_scatter | solution.py:96
  335.2 47.3 %reduce-scatter.7.cloned.1.call-done = bf16[128,1024]{0,1:T(8,128)(2,1)} async-done(((bf16[128,8192]{0,1:T(8,128)(2,1)}), bf16[128,1024]{0,1:T(8,128)(2,1)}) %reduce-scatter.7.cloned.1.call-update) | async-done | bytes 262160 | tf_op jit(solution)/shard_map/reduce_scatter | solution.py:79
  384.2 42.1 %reduce-scatter.5.cloned.1.call-done = bf16[128,1024]{0,1:T(8,128)(2,1)} async-done(((bf16[128,8192]{0,1:T(8,128)(2,1)}), bf16[128,1024]{0,1:T(8,128)(2,1)}) %reduce-scatter.5.cloned.1.call-update) | async-done | bytes 262160 | tf_op jit(solution)/shard_map/reduce_scatter | solution.py:66
  428.1 40.7 %all-reduce.3.cloned.1.call-done = (bf16[8,128,128]{2,1,0:T(8,128)(2,1)}, bf16[8,128,128]{2,1,0:T(8,128)(2,1)}) async-done(((bf16[8,128,128]{2,1,0:T(8,128)(2,1)}, bf16[8,128,128]{2,1,0:T(8,128)(2,1)}), (bf16[8,128,128]{2,1,0:T(8,128)(2,1)}, bf16[8,128,128]{2,1,0:T(8,128)(2,1)})) %all-reduce.3.cloned.1.call-update) | async-done | bytes 524304 | tf_op jit(solution)/shard_map/psum | solution.py:101
  (62 shorter events, 52.6 us)
Async XLA Ops:
  7.2 10.9 %copy-start = (s32[128,1]{0,1:T(1,128)S(1)}, s32[128,1]{0,1:T(1,128)}, u32[]{:S(2)}) copy-start(s32[128,1]{0,1:T(1,128)} %param.12) | copy-start | bytes 1540
  7.2 48.0 %all-gather.9.cloned.1.call-start = ((), (), s32[]{:S(2)}) async-start(), calls=%async_computation.6 | async-start | bytes 2359296 | tf_op jit(solution)/shard_map/all_gather | solution.py:51
  9.0 88.1 %all-gather.11.cloned.1.call-start = ((), (), s32[]{:S(2)}) async-start(), calls=%async_computation.8 | async-start | bytes 2359296 | tf_op jit(solution)/shard_map/all_gather | solution.py:69
  10.9 126.3 %all-gather.7.cloned.1.call-start = ((), (), s32[]{:S(2)}) async-start(), calls=%async_computation.5 | async-start | bytes 4456448 | tf_op jit(solution)/shard_map/all_gather | solution.py:53
  11.7 167.3 %all-gather.5.cloned.1.call-start = ((), (), s32[]{:S(2)}) async-start(), calls=%async_computation.4 | async-start | bytes 4456448 | tf_op jit(solution)/shard_map/all_gather | solution.py:60
  12.2 306.9 %reduce-scatter.9.cloned.1.call-start = ((), (), s32[]{:S(2)}) async-start(), calls=%async_computation.10 | async-start | bytes 4456448 | tf_op jit(solution)/shard_map/reduce_scatter | solution.py:93
  184.2 5.0 %copy-start.2 = (bf16[128,128,128]{2,1,0:T(8,128)(2,1)S(1)}, bf16[128,128,128]{2,1,0:T(8,128)(2,1)}, u32[]{:S(2)}) copy-start(bf16[128,128,128]{2,1,0:T(8,128)(2,1)} %gather_fusion.4) | copy-start | bytes 12582916
  197.7 137.4 %reduce-scatter.11.cloned.1.call-start = ((), (), s32[]{:S(2)}) async-start(), calls=%async_computation.11 | async-start | bytes 4456448 | tf_op jit(solution)/shard_map/reduce_scatter | solution.py:96
  217.8 164.6 %reduce-scatter.7.cloned.1.call-start = ((), (), s32[]{:S(2)}) async-start(), calls=%async_computation.9 | async-start | bytes 2359296 | tf_op jit(solution)/shard_map/reduce_scatter | solution.py:79
  268.3 158.0 %reduce-scatter.5.cloned.1.call-start = ((), (), s32[]{:S(2)}) async-start(), calls=%async_computation.7 | async-start | bytes 2359296 | tf_op jit(solution)/shard_map/reduce_scatter | solution.py:66
  313.5 158.8 %copy-start.1 = (s32[128,1]{0,1:T(1,128)S(1)}, s32[128,1]{0,1:T(1,128)}, u32[]{:S(2)}) copy-start(s32[128,1]{0,1:T(1,128)} %param.12) | copy-start | bytes 1540
  319.1 149.7 %all-reduce.3.cloned.1.call-start = ((), (), s32[]{:S(2)}) async-start(), calls=%async_computation.12 | async-start | bytes 1048576 | tf_op jit(solution)/shard_map/psum | solution.py:101
Sparse Core Ops, SparseCore 0:
  10.4 44.7 all-gather.8
  57.5 39.5 all-gather.10
  99.0 38.2 all-gather.6
  139.0 39.9 all-gather.4
  197.9 66.1 reduce-scatter.8
  266.5 68.6 reduce-scatter.10
  337.7 44.6 reduce-scatter.6
  385.0 41.2 reduce-scatter.4
  428.9 39.7 all-reduce.2
where the time goes:
time: 482 us; the launch traced here: 479 us
  waiting for transfers between devices  277 us (57%)
  local copies, waits for them, and re-layouts  81.1 us (17%)
  other arithmetic  73.8 us (15%)
  matrix products  32.2 us (7%)
  between operations  14 us (3%)
    scatter-add x2, other arithmetic, add_far(): jnp.zeros((rows_here, model_blocks, block_size), jnp.float32)  53.5 us
    reduce_scatter x1, waiting for transfers between devices, body(): lax.psum_scatter(partial_in.astype(jnp.bfloat16), 'tensor', scatter_dimen...  47.3 us
    reduce_scatter x1, waiting for transfers between devices, body(): lax.psum_scatter(partial_out.astype(jnp.bfloat16), 'tensor', scatter_dime...  42.1 us
    psum x1, waiting for transfers between devices, body(): lax.psum(up_part.astype(jnp.bfloat16), 'dp').astype(jnp.float32)  40.7 us
    all_gather x1, waiting for transfers between devices, body(): full_cotangent = lax.all_gather(cotangent, 'tensor', axis=1, tiled=True)  38.7 us
    all_gather x1, waiting for transfers between devices, body(): down_whole = lax.all_gather(down_tiles, 'fsdp', axis=0, tiled=True)  31.7 us
    all_gather x1, waiting for transfers between devices, body(): full_input = lax.all_gather(activations, 'tensor', axis=1, tiled=True)  31 us
    all_gather x1, waiting for transfers between devices, body(): up_whole = lax.all_gather(up_tiles, 'fsdp', axis=0, tiled=True)  28.4 us
  transfers between devices with their start and end apart: 9, of which 8 were waited for; matrix products, arithmetic and copies ran while one was open for 34% of the time, Pallas kernels for 0%

commit v1 on v0

v1 whole, which is shorter than its diff:
```python
import functools

import jax
import jax.numpy as jnp
from jax import lax
from jax.experimental import pallas as pl
from jax.experimental.pallas import tpu as pltpu
from jax.sharding import PartitionSpec as P

BF = jnp.bfloat16
F32 = jnp.float32
inv_root_two = 0.7071067811865476
inv_root_tau = 0.3989422804014327

B = 128
H = 16
K = 8
NT = 128
VMEM_LIMIT = 56 * 1024 * 1024

SMEM_SPEC = pl.BlockSpec(memory_space=pltpu.SMEM)
VMEM_SPEC = pl.BlockSpec(memory_space=pltpu.VMEM)
ANY_SPEC = pl.BlockSpec(memory_space=pl.ANY)


def gelu_parts(values):
    normal_cdf = 0.5 * (1.0 + lax.erf(values * inv_root_two))
    density = inv_root_tau * jnp.exp(-0.5 * values * values)
    return (values * normal_cdf, normal_cdf + values * density)


def dot(a, b, dims):
    return lax.dot_general(a, b, ((dims[:1], dims[1:]), ((), ())), preferred_element_type=F32)


def plan_kernel(cols_ref, rows_ref, up_ref, down_ref, count):
    for near, order in ((cols_ref, up_ref), (rows_ref, down_ref)):
        for h in range(H):
            count[h] = 0

        def step(j, carry):
            h = near[j]
            c = count[h]
            order[h * K + c] = j
            count[h] = c + 1
            return carry

        lax.fori_loop(0, NT, step, 0)


def plan(cols, rows):
    shape = jax.ShapeDtypeStruct((NT,), jnp.int32)
    return pl.pallas_call(
        plan_kernel,
        out_shape=(shape, shape),
        in_specs=[SMEM_SPEC] * 2,
        out_specs=(SMEM_SPEC, SMEM_SPEC),
        scratch_shapes=[pltpu.SMEM((H,), jnp.int32)],
        name="plan",
    )(cols, rows)


def block(ref, f):
    return ref[f // 8, :, pl.ds(pl.multiple_of((f % 8) * B, B), B)]


class Wide:
    def __init__(self, arrays, places):
        self.arrays, self.places = arrays, places


def wide_copies(places, refs, pos, buf, sems, first):
    copies = []
    for n, (which, index, shift) in enumerate(places):
        slot = shift if isinstance(shift, int) else lax.rem(pos[0] + shift[0] + 8, 8)
        src = refs[which].at[index] if index is not None else refs[which]
        copies.append(pltpu.make_async_copy(src, buf.at[slot], sems.at[first + n]))
    return copies


def tile_copies(places, refs, pos, buf, sems, first):
    copies = []
    for n, (which, index, (dx, dy, dc)) in enumerate(places):
        slot = (
            lax.rem(pos[1] - dx + 4, 4) * 4
            + lax.rem(pos[2] + dy, 2) * 2
            + lax.rem(pos[3] + dc, 2)
        )
        src = refs[which].at[index] if index is not None else refs[which]
        copies.append(
            pltpu.make_async_copy(src, buf.at[pl.ds(slot * 8, 8)], sems.at[first + n])
        )
    return copies


WIDE = pltpu.VMEM((8, B, 8 * B), BF)
TILES = pltpu.VMEM((NT, B, B), BF)
WIDE_ACC = pltpu.VMEM((8, B, 8 * B), F32)


def call(kernel, out_shape, smem, hbm, vmem, scratch, out_specs=None, name=None):
    n_out = len(out_shape)
    return pl.pallas_call(
        kernel,
        out_shape=tuple(out_shape),
        in_specs=[SMEM_SPEC] * len(smem) + [ANY_SPEC] * len(hbm) + [VMEM_SPEC] * len(vmem),
        out_specs=out_specs or (VMEM_SPEC,) * n_out,
        scratch_shapes=scratch,
        compiler_params=pltpu.CompilerParams(vmem_limit_bytes=VMEM_LIMIT),
        name=name,
    )(*smem, *hbm, *vmem)


def start(copies):
    for c in copies:
        c.start()


def finish(copies):
    for c in copies:
        c.wait()


def far_blocks(buf, rows, order, h):
    return jnp.concatenate([block(buf, rows[order[h * K + k]]) for k in range(K)], axis=1)


def forward(order, rows, pos, x, w):
    def kernel(order, rows, pos, *refs):
        x_refs, w_refs = refs[: len(x.arrays)], refs[len(x.arrays) : len(x.arrays) + len(w.arrays)]
        hidden, slope, xbuf, wbuf, sems = refs[len(x.arrays) + len(w.arrays) :]
        copies = wide_copies(x.places, x_refs, pos, xbuf, sems, 0)
        copies += tile_copies(w.places, w_refs, pos, wbuf, sems, len(x.places))
        start(copies)
        finish(copies)

        def step(h, carry):
            lhs = far_blocks(xbuf, rows, order, h)
            rhs = jnp.concatenate([wbuf[order[h * K + k]] for k in range(K)], axis=0)
            act, der = gelu_parts(dot(lhs, rhs, (1, 0)))
            hidden[h] = act.astype(BF)
            slope[h] = der
            return carry

        lax.fori_loop(0, H, step, 0)

    return call(
        kernel,
        (jax.ShapeDtypeStruct((H, B, B), BF), jax.ShapeDtypeStruct((H, B, B), F32)),
        (order, rows, pos),
        (*x.arrays, *w.arrays),
        (),
        [WIDE, TILES, pltpu.SemaphoreType.DMA((len(x.places) + len(w.places),))],
        name="forward",
    )


GRADS = jax.ShapeDtypeStruct((2, 4, 2, 8, B, B), BF)


def grad_place(j, pos):
    owner = j // 8
    dx = lax.rem(owner // 4 - pos[1] + 4, 4)
    dy = lax.rem(lax.rem(owner // 2, 2) + pos[2], 2)
    dc = lax.rem(lax.rem(owner, 2) + pos[3], 2)
    return dc, dx, dy, lax.rem(j, 8)


def down_grads(order, cols, pos, hidden, cot):
    def kernel(order, cols, pos, *refs):
        n = len(cot.arrays)
        c_refs = refs[:n]
        hid, grads, cbuf, sems = refs[n:]
        copies = wide_copies(cot.places, c_refs, pos, cbuf, sems, 0)
        start(copies)
        finish(copies)

        def step(h, carry):
            term = dot(hid[h], far_blocks(cbuf, cols, order, h), (0, 0)).astype(BF)
            for k in range(K):
                grads[grad_place(order[h * K + k], pos)] = term[:, k * B : (k + 1) * B]
            return carry

        lax.fori_loop(0, H, step, 0)

    return call(
        kernel,
        (GRADS,),
        (order, cols, pos),
        cot.arrays,
        (hidden,),
        [WIDE, pltpu.SemaphoreType.DMA((len(cot.places),))],
        name="down_grads",
    )[0]


def pre_grads(down_order, cols, up_order, rows, pos, slope, cot, w, x):
    def kernel(down_order, cols, up_order, rows, pos, *refs):
        nc, nw, nx = len(cot.arrays), len(w.arrays), len(x.arrays)
        c_refs, w_refs, x_refs = refs[:nc], refs[nc : nc + nw], refs[nc + nw : nc + nw + nx]
        slope, pre, grads, cbuf, wbuf, xbuf, sems = refs[nc + nw + nx :]
        first = wide_copies(cot.places, c_refs, pos, cbuf, sems, 0)
        first += tile_copies(w.places, w_refs, pos, wbuf, sems, len(first))
        later = wide_copies(x.places, x_refs, pos, xbuf, sems, len(first))
        start(first)
        start(later)
        finish(first)

        def step(h, carry):
            lhs = far_blocks(cbuf, cols, down_order, h)
            rhs = jnp.concatenate([wbuf[down_order[h * K + k]] for k in range(K)], axis=1)
            pre[h] = (dot(lhs, rhs, (1, 1)) * slope[h]).astype(BF)
            return carry

        lax.fori_loop(0, H, step, 0)
        finish(later)

        def term(h, carry):
            lhs = far_blocks(xbuf, rows, up_order, h)
            out = dot(lhs, pre[h], (0, 0)).astype(BF)
            for k in range(K):
                grads[grad_place(up_order[h * K + k], pos)] = out[k * B : (k + 1) * B]
            return carry

        lax.fori_loop(0, H, term, 0)

    n = len(cot.places) + len(w.places) + len(x.places)
    return call(
        kernel,
        (jax.ShapeDtypeStruct((H, B, B), BF), GRADS),
        (down_order, cols, up_order, rows, pos),
        (*cot.arrays, *w.arrays, *x.arrays),
        (slope,),
        [WIDE, TILES, WIDE, pltpu.SemaphoreType.DMA((n,))],
        name="pre_grads",
    )


def spread(order, far, pos, act, w, transposed, name):
    def kernel(order, far, pos, *refs):
        nw = len(w.arrays)
        act, out, wbuf, acc, sems = refs[nw:]
        copies = tile_copies(w.places, refs[:nw], pos, wbuf, sems, 0)
        start(copies)
        acc[...] = jnp.zeros_like(acc)
        finish(copies)

        def step(h, carry):
            js = [order[h * K + k] for k in range(K)]
            axis = 0 if transposed else 1
            rhs = jnp.concatenate([wbuf[j] for j in js], axis=axis)
            term = dot(act[h], rhs, (1, 1 - axis))
            for k, j in enumerate(js):
                f = far[j]
                at = (f // 8, slice(None), pl.ds(pl.multiple_of((f % 8) * B, B), B))
                acc[at] += term[:, k * B : (k + 1) * B]
            return carry

        lax.fori_loop(0, H, step, 0)
        out[...] = acc[...].astype(BF)

    return call(
        kernel,
        (jax.ShapeDtypeStruct((8, B, 8 * B), BF),),
        (order, far, pos),
        w.arrays,
        (act,),
        [TILES, WIDE_ACC, pltpu.SemaphoreType.DMA((len(w.places),))],
        name=name,
    )[0]


def core_swap(a):
    return lax.ppermute(a, "fsdp", [(i, i ^ 1) for i in range(16)])


def y_swap(a):
    return lax.ppermute(a, "fsdp", [(i, i ^ 2) for i in range(16)])


def x_shift(a, d):
    return lax.ppermute(a, "fsdp", [(i, (i + 4 * d) % 16) for i in range(16)])


def dp_swap(a):
    return lax.ppermute(a, "dp", [(0, 1), (1, 0)])


def gather_tiles(tiles):
    both = jnp.stack([tiles, y_swap(tiles)])
    mine = [both] + [x_shift(both, d) for d in (1, 2, 3)]
    theirs = [core_swap(a) for a in mine]
    arrays, places = [], []
    for dc, group in enumerate((mine, theirs)):
        for dx, a in enumerate(group):
            for dy in range(2):
                places.append((len(arrays), dy, (dx, dy, dc)))
            arrays.append(a)
    return Wide(tuple(arrays), places)


def reduce_tiles(grads):
    sums = []
    for dx in range(4):
        got = core_swap(grads[1, dx])
        sums.append(grads[0, dx].astype(F32) + got.astype(F32))
    total = sums[0]
    for dx in (1, 2, 3):
        total = total + x_shift(sums[dx].astype(BF), dx).astype(F32)
    part = total[0] + y_swap(total[1].astype(BF)).astype(F32)
    part = part.astype(BF)
    return part.astype(F32) + dp_swap(part).astype(F32)


def scatter_features(partial):
    return lax.psum_scatter(partial, "tensor", scatter_dimension=0, tiled=True)[0]


def body(activations, cotangent, up_tiles, down_tiles, up_rows, up_cols, down_rows, down_cols):
    f = lax.axis_index("fsdp")
    pos = jnp.stack([lax.axis_index("tensor"), f // 4, (f // 2) % 2, f % 2]).astype(jnp.int32)
    rows, cols = up_rows[:, 0], down_cols[:, 0]
    up_order, down_order = plan(up_cols[:, 0], down_rows[:, 0])
    pair = lax.all_gather(jnp.stack([activations, cotangent]), "tensor", axis=0, tiled=False)
    x = Wide((pair,), [(0, (z, 0), z) for z in range(8)])
    cot = Wide((pair,), [(0, (z, 1), z) for z in range(8)])
    up = gather_tiles(up_tiles)
    down = gather_tiles(down_tiles)
    hidden, slope = forward(up_order, rows, pos, x, up)
    down_term = down_grads(down_order, cols, pos, hidden, cot)
    pre_grad, up_term = pre_grads(down_order, cols, up_order, rows, pos, slope, cot, down, x)
    partial_out = spread(down_order, cols, pos, hidden, down, False, "out_part")
    partial_in = spread(up_order, rows, pos, pre_grad, up, True, "in_part")
    output = scatter_features(partial_out)
    input_grad = scatter_features(partial_in)
    return (output, input_grad, reduce_tiles(up_term), reduce_tiles(down_term))


def solution(mesh):
    in_specs = (
        P(("dp", "fsdp"), "tensor"),
        P(("dp", "fsdp"), "tensor"),
        P(("fsdp", "tensor"), None, None),
        P(("fsdp", "tensor"), None, None),
        P(None, "tensor"),
        P(None, "tensor"),
        P(None, "tensor"),
        P(None, "tensor"),
    )
    out_specs = (
        P(("dp", "fsdp"), "tensor"),
        P(("dp", "fsdp"), "tensor"),
        P(("fsdp", "tensor"), None, None),
        P(("fsdp", "tensor"), None, None),
    )
    return jax.shard_map(body, mesh=mesh, in_specs=in_specs, out_specs=out_specs, check_vma=False)
```

time: 482 us -> 215 us (0.45)
  waiting for transfers between devices: 277 us -> 95.9 us
  local copies, waits for them, and re-layouts: 81.1 us -> 4.38 us
  other arithmetic: 73.8 us -> 8.41 us
  Pallas kernels: 0 us -> 57.2 us
  starting transfers between devices: 0.55 us -> 33.2 us
  matrix products: 32.2 us -> 0 us
    all_gather x4 -> x1, waiting for transfers between devices: 130 us -> 0.01 us  [body(): lax.all_gather(jnp.stack([activations, cotangent]), 'tensor', axis=0, til...]
    reduce_scatter x4 -> x2, waiting for transfers between devices: 105 us -> 0.01 us  [scatter_features(): lax.psum_scatter(partial, 'tensor', scatter_dimension=0, tiled=True)[0]]
    ppermute x0 -> x34, waiting for transfers between devices: none -> 95.9 us  [the longest x12 74 us: x_shift(): return lax.ppermute(a, 'fsdp', [(i, (i + 4 * d) % 16) for i in range(16)])]
    pallas_call x0 -> x6, Pallas kernels: none -> 57.2 us  [the longest x5 52.6 us: call(): pl.pallas_call(kernel, out_shape=tuple(out_shape), in_specs=[SMEM_SPEC] *...]
    scatter-add x2 -> x0, other arithmetic: 53.5 us -> none  [add_far(): jnp.zeros((rows_here, model_blocks, block_size), jnp.float32)]
    psum x1 -> x0, waiting for transfers between devices: 40.7 us -> none  [body(): lax.psum(up_part.astype(jnp.bfloat16), 'dp').astype(jnp.float32)]
    ppermute x0 -> x34, starting transfers between devices: none -> 32.9 us  [the longest x12 20.8 us: x_shift(): return lax.ppermute(a, 'fsdp', [(i, (i + 4 * d) % 16) for i in range(16)])]
    dot_general x6 -> x0, matrix products: 32.2 us -> none  [the longest x1 6.78 us: body(): jnp.einsum('thb,hkbc->thkc', hidden, down_sorted, preferred_element_type=...]
  transfers between devices with their start and end apart: 9 -> 37, of which waited for: 8 -> 13; matrix products, arithmetic and copies ran while one was open for 34% -> 5% of each run, Pallas kernels for 0% -> 22%
where the time goes in v1:
time: 215 us; the launch traced here: 213 us
  waiting for transfers between devices  95.9 us (45%)
  Pallas kernels  57.2 us (27%)
  starting transfers between devices  33.2 us (15%)
  between operations  14 us (7%)
  other arithmetic  8.41 us (4%)
  local copies, waits for them, and re-layouts  4.38 us (2%)
    ppermute x12, waiting for transfers between devices, x_shift(): return lax.ppermute(a, 'fsdp', [(i, (i + 4 * d) % 16) for i in range(16)])  74 us
    pallas_call x5, Pallas kernels, call(): pl.pallas_call(kernel, out_shape=tuple(out_shape), in_specs=[SMEM_SPEC] *...  52.6 us
    ppermute x12, starting transfers between devices, x_shift(): return lax.ppermute(a, 'fsdp', [(i, (i + 4 * d) % 16) for i in range(16)])  20.8 us
    ppermute x4, waiting for transfers between devices, y_swap(): return lax.ppermute(a, 'fsdp', [(i, i ^ 2) for i in range(16)])  13.2 us
    ppermute x2, waiting for transfers between devices, dp_swap(): return lax.ppermute(a, 'dp', [(0, 1), (1, 0)])  7.86 us
    ppermute x2, starting transfers between devices, dp_swap(): return lax.ppermute(a, 'dp', [(0, 1), (1, 0)])  5.25 us
    pallas_call x1, Pallas kernels, plan(): pl.pallas_call(plan_kernel, out_shape=(shape, shape), in_specs=[SMEM_SPEC...  4.58 us
  transfers between devices with their start and end apart: 37, of which 13 were waited for; matrix products, arithmetic and copies ran while one was open for 5% of the time, Pallas kernels for 22%

profile of v1, /device:TPU:8, one launch (start us, length us, event | category | flops | bytes accessed | tf_op | source)
XLA Modules:
  0.0 213.1 jit_solution(15422084110517508843)
XLA Ops:
  9.1 2.3 %collective-permute-start = (bf16[8,128,128]{2,1,0:T(8,128)(2,1)}, bf16[8,128,128]{2,1,0:T(8,128)(2,1)S(1)}, u32[]{:S(2)}, u32[]{:S(2)}) collective-permute-start(bf16[8,128,128]{2,1,0:T(8,128)(2,1)} %param.11), channel_id=1, source_target_pairs={{0,16},{8,24},{16,0},{24,8},{32,48},{40,56},{48,32},{56,40},{64,80... | collective-permute-start | bytes 786440 | tf_op jit(solution)/shard_map/ppermute | solution.py:278
  11.5 7.3 %collective-permute-done = bf16[8,128,128]{2,1,0:T(8,128)(2,1)S(1)} collective-permute-done((bf16[8,128,128]{2,1,0:T(8,128)(2,1)}, bf16[8,128,128]{2,1,0:T(8,128)(2,1)S(1)}, u32[]{:S(2)}, u32[]{:S(2)}) %collective-permute-start) | collective-permute-done | bytes 262176 | tf_op jit(solution)/shard_map/ppermute | solution.py:278
  21.2 2.7 %collective-permute-start.2 = (bf16[2,8,128,128]{3,2,1,0:T(8,128)(2,1)S(1)}, bf16[2,8,128,128]{3,2,1,0:T(8,128)(2,1)S(1)}, u32[]{:S(2)}, u32[]{:S(2)}) collective-permute-start(bf16[2,8,128,128]{3,2,1,0:T(8,128)(2,1)S(1)} %pad_maximum_fusion.refs_0_.refs_1_), channel_id=1, source_target_pairs={{0,64},{8,72},{16,80},{24,88},{32,96},{40,104},{48,112},{56,120},{... | collective-permute-start | bytes 1572872 | tf_op jit(solution)/shard_map/ppermute | solution.py:282
  25.7 2.7 %collective-permute-start.10 = (bf16[2,8,128,128]{3,2,1,0:T(8,128)(2,1)S(1)}, bf16[2,8,128,128]{3,2,1,0:T(8,128)(2,1)S(1)}, u32[]{:S(2)}, u32[]{:S(2)}) collective-permute-start(bf16[2,8,128,128]{3,2,1,0:T(8,128)(2,1)S(1)} %pad_maximum_fusion.2.refs_1_.refs_0_), channel_id=1, source_target_pairs={{0,64},{8,72},{16,80},{24,88},{32,96},{40,104},{48,112},{56,120},{... | collective-permute-start | bytes 1572872 | tf_op jit(solution)/shard_map/ppermute | solution.py:282
  29.9 16.5 %collective-permute-done.1.refs_1_.refs_2_ = bf16[2,8,128,128]{3,2,1,0:T(8,128)(2,1)S(1)} collective-permute-done((bf16[2,8,128,128]{3,2,1,0:T(8,128)(2,1)S(1)}, bf16[2,8,128,128]{3,2,1,0:T(8,128)(2,1)S(1)}, u32[]{:S(2)}, u32[]{:S(2)}) %collective-permute-start.1) | collective-permute-done | bytes 524320 | tf_op jit(solution)/shard_map/ppermute | solution.py:282
  48.1 8.8 %collective-permute-done.9.refs_2_.refs_1_ = bf16[2,8,128,128]{3,2,1,0:T(8,128)(2,1)S(1)} collective-permute-done((bf16[2,8,128,128]{3,2,1,0:T(8,128)(2,1)S(1)}, bf16[2,8,128,128]{3,2,1,0:T(8,128)(2,1)S(1)}, u32[]{:S(2)}, u32[]{:S(2)}) %collective-permute-start.9) | collective-permute-done | bytes 524320 | tf_op jit(solution)/shard_map/ppermute | solution.py:282
  56.9 10.5 %collective-permute-done.10.refs_3_.refs_2_ = bf16[2,8,128,128]{3,2,1,0:T(8,128)(2,1)S(1)} collective-permute-done((bf16[2,8,128,128]{3,2,1,0:T(8,128)(2,1)S(1)}, bf16[2,8,128,128]{3,2,1,0:T(8,128)(2,1)S(1)}, u32[]{:S(2)}, u32[]{:S(2)}) %collective-permute-start.10) | collective-permute-done | bytes 524320 | tf_op jit(solution)/shard_map/ppermute | solution.py:282
  70.0 4.6 %plan.1 = (s32[128]{0:T(128)}, s32[128]{0:T(128)}) custom-call(s32[128]{0:T(128)} %bitcast.99, s32[128]{0:T(128)} %bitcast.100), custom_call_target="tpu_custom_call" | custom-call | tf_op jit(solution)/shard_map/plan/pallas_call | solution.py:53
  75.2 8.8 %forward.1 = (bf16[16,128,128]{2,1,0:T(8,128)(2,1)}, f32[16,128,128]{2,1,0:T(8,128)}) custom-call(s32[128]{0:T(128)} %get-tuple-element.11.order.up_order, s32[128]{0:T(128)} %bitcast.91, s32[4]{0:T(128)} %pad_add_fusion.pos, bf16[8,2,128,1024]{3,2,1,0:T(8,128)(2,1)} %bitcast.81, bf16[2,8,128,128]{3,2,1,0:T(8,128)(2,1)} %copy-done.2, ...), custom_call_target="tpu_custom_call" | custom-call | tf_op jit(solution)/shard_map/forward/pallas_call | solution.py:103
  84.1 9.2 %out_part.1 = bf16[8,128,1024]{2,1,0:T(8,128)(2,1)} custom-call(s32[128]{0:T(128)} %get-tuple-element.10.order.down_order, s32[128]{0:T(128)} %bitcast.94, s32[4]{0:T(128)} %pad_add_fusion.pos, bf16[2,8,128,128]{3,2,1,0:T(8,128)(2,1)} %copy-done.1, bf16[2,8,128,128]{3,2,1,0:T(8,128)(2,1)} %copy-done.4, bf16[2,8,128,128]{3,2,1,0:T(8,128)(2,1)} %copy-done.5, ...), custom_call_target="tpu_custom_call" | custom-call | tf_op jit(solution)/shard_map/out_part/pallas_call | solution.py:103
  93.6 15.4 %pre_grads.1 = (bf16[16,128,128]{2,1,0:T(8,128)(2,1)}, bf16[2,4,2,8,128,128]{5,4,3,2,1,0:T(8,128)(2,1)}) custom-call(s32[128]{0:T(128)} %get-tuple-element.10.order.down_order, s32[128]{0:T(128)} %bitcast.95, s32[128]{0:T(128)} %get-tuple-element.11.order.up_order, s32[128]{0:T(128)} %bitcast.92, s32[4]{0:T(128)} %pad_add_fusion.pos, ...), custom_call_target="tpu_custom_call" | custom-call | tf_op jit(solution)/shard_map/pre_grads/pallas_call | solution.py:103
  109.0 9.4 %in_part.1 = bf16[8,128,1024]{2,1,0:T(8,128)(2,1)} custom-call(s32[128]{0:T(128)} %get-tuple-element.11.order.up_order, s32[128]{0:T(128)} %bitcast.93, s32[4]{0:T(128)} %pad_add_fusion.pos, bf16[2,8,128,128]{3,2,1,0:T(8,128)(2,1)} %copy-done.2, bf16[2,8,128,128]{3,2,1,0:T(8,128)(2,1)} %copy-done.6, bf16[2,8,128,128]{3,2,1,0:T(8,128)(2,1)} %copy-done.7, ...), custom_call_target="tpu_custom_call" | custom-call | tf_op jit(solution)/shard_map/in_part/pallas_call | solution.py:103
  121.0 9.7 %down_grads.1 = bf16[2,4,2,8,128,128]{5,4,3,2,1,0:T(8,128)(2,1)} custom-call(s32[128]{0:T(128)} %get-tuple-element.10.order.down_order, s32[128]{0:T(128)} %bitcast.96, s32[4]{0:T(128)} %pad_add_fusion.pos, bf16[8,2,128,1024]{3,2,1,0:T(8,128)(2,1)} %bitcast.84, bf16[16,128,128]{2,1,0:T(8,128)(2,1)} %get-tuple-element.12.refs_8_.refs_1_), custom_call_target="tpu_custom_call" | custom-call | tf_op jit(solution)/shard_map/down_grads/pallas_call | solution.py:103
  138.7 3.2 %collective-permute-start.31 = (bf16[2,8,128,128]{3,2,1,0:T(8,128)(2,1)S(1)}, bf16[2,8,128,128]{3,2,1,0:T(8,128)(2,1)S(1)}, u32[]{:S(2)}, u32[]{:S(2)}) collective-permute-start(bf16[2,8,128,128]{3,2,1,0:T(8,128)(2,1)S(1)} %get-tuple-element.21), channel_id=1, source_target_pairs={{0,96},{8,104},{16,112},{24,120},{32,0},{40,8},{48,16},{56,24},{64... | collective-permute-start | bytes 1572872 | tf_op jit(solution)/shard_map/ppermute | solution.py:282
  141.9 17.0 %collective-permute-done.22 = bf16[2,8,128,128]{3,2,1,0:T(8,128)(2,1)S(1)} collective-permute-done((bf16[2,8,128,128]{3,2,1,0:T(8,128)(2,1)S(1)}, bf16[2,8,128,128]{3,2,1,0:T(8,128)(2,1)S(1)}, u32[]{:S(2)}, u32[]{:S(2)}) %collective-permute-start.22) | collective-permute-done | bytes 524320 | tf_op jit(solution)/shard_map/ppermute | solution.py:282
  160.8 3.2 %collective-permute-start.27 = (bf16[2,8,128,128]{3,2,1,0:T(8,128)(2,1)S(1)}, bf16[2,8,128,128]{3,2,1,0:T(8,128)(2,1)S(1)}, u32[]{:S(2)}, u32[]{:S(2)}) collective-permute-start(bf16[2,8,128,128]{3,2,1,0:T(8,128)(2,1)S(1)} %get-tuple-element.20), channel_id=1, source_target_pairs={{0,32},{8,40},{16,48},{24,56},{32,64},{40,72},{48,80},{56,88},{64,... | collective-permute-start | bytes 1572872 | tf_op jit(solution)/shard_map/ppermute | solution.py:282
  165.2 6.4 %collective-permute-done.31 = bf16[2,8,128,128]{3,2,1,0:T(8,128)(2,1)S(1)} collective-permute-done((bf16[2,8,128,128]{3,2,1,0:T(8,128)(2,1)S(1)}, bf16[2,8,128,128]{3,2,1,0:T(8,128)(2,1)S(1)}, u32[]{:S(2)}, u32[]{:S(2)}) %collective-permute-start.31) | collective-permute-done | bytes 524320 | tf_op jit(solution)/shard_map/ppermute | solution.py:282
  171.6 3.7 %collective-permute-done.29 = bf16[2,8,128,128]{3,2,1,0:T(8,128)(2,1)S(1)} collective-permute-done((bf16[2,8,128,128]{3,2,1,0:T(8,128)(2,1)S(1)}, bf16[2,8,128,128]{3,2,1,0:T(8,128)(2,1)S(1)}, u32[]{:S(2)}, u32[]{:S(2)}) %collective-permute-start.29) | collective-permute-done | bytes 524320 | tf_op jit(solution)/shard_map/ppermute | solution.py:282
  175.3 9.4 %collective-permute-done.27 = bf16[2,8,128,128]{3,2,1,0:T(8,128)(2,1)S(1)} collective-permute-done((bf16[2,8,128,128]{3,2,1,0:T(8,128)(2,1)S(1)}, bf16[2,8,128,128]{3,2,1,0:T(8,128)(2,1)S(1)}, u32[]{:S(2)}, u32[]{:S(2)}) %collective-permute-start.27) | collective-permute-done | bytes 524320 | tf_op jit(solution)/shard_map/ppermute | solution.py:282
  185.8 2.8 %collective-permute-start.24 = (bf16[8,128,128]{2,1,0:T(8,128)(2,1)S(1)}, bf16[8,128,128]{2,1,0:T(8,128)(2,1)S(1)}, u32[]{:S(2)}, u32[]{:S(2)}) collective-permute-start(bf16[8,128,128]{2,1,0:T(8,128)(2,1)S(1)} %fusion.15), channel_id=1, source_target_pairs={{0,128},{128,0},{1,129},{129,1},{2,130},{130,2},{3,131},{131,3},{4... | collective-permute-start | bytes 786440 | tf_op jit(solution)/shard_map/ppermute | solution.py:286
  188.6 5.9 %collective-permute-done.32 = bf16[8,128,128]{2,1,0:T(8,128)(2,1)S(1)} collective-permute-done((bf16[8,128,128]{2,1,0:T(8,128)(2,1)S(1)}, bf16[8,128,128]{2,1,0:T(8,128)(2,1)S(1)}, u32[]{:S(2)}, u32[]{:S(2)}) %collective-permute-start.32) | collective-permute-done | bytes 262176 | tf_op jit(solution)/shard_map/ppermute | solution.py:278
  194.6 2.5 %collective-permute-start.33 = (bf16[8,128,128]{2,1,0:T(8,128)(2,1)S(1)}, bf16[8,128,128]{2,1,0:T(8,128)(2,1)S(1)}, u32[]{:S(2)}, u32[]{:S(2)}) collective-permute-start(bf16[8,128,128]{2,1,0:T(8,128)(2,1)S(1)} %fusion.13), channel_id=1, source_target_pairs={{0,128},{128,0},{1,129},{129,1},{2,130},{130,2},{3,131},{131,3},{4... | collective-permute-start | bytes 786440 | tf_op jit(solution)/shard_map/ppermute | solution.py:286
  197.1 4.2 %collective-permute-done.24 = bf16[8,128,128]{2,1,0:T(8,128)(2,1)S(1)} collective-permute-done((bf16[8,128,128]{2,1,0:T(8,128)(2,1)S(1)}, bf16[8,128,128]{2,1,0:T(8,128)(2,1)S(1)}, u32[]{:S(2)}, u32[]{:S(2)}) %collective-permute-start.24) | collective-permute-done | bytes 262176 | tf_op jit(solution)/shard_map/ppermute | solution.py:286
  202.1 3.7 %collective-permute-done.33 = bf16[8,128,128]{2,1,0:T(8,128)(2,1)S(1)} collective-permute-done((bf16[8,128,128]{2,1,0:T(8,128)(2,1)S(1)}, bf16[8,128,128]{2,1,0:T(8,128)(2,1)S(1)}, u32[]{:S(2)}, u32[]{:S(2)}) %collective-permute-start.33) | collective-permute-done | bytes 262176 | tf_op jit(solution)/shard_map/ppermute | solution.py:286
  (97 shorter events, 29.2 us)
Async XLA Ops:
  7.2 68.0 %all-gather.3.cloned.1.call-start = ((), (), s32[]{:S(2)}) async-start(), calls=%async_computation.4 | async-start | bytes 4718592 | tf_op jit(solution)/shard_map/all_gather | solution.py:324
  9.1 197.5 %reduce-scatter.3.cloned.1.call-start = ((), (), s32[]{:S(2)}) async-start(), calls=%async_computation.2 | async-start | bytes 2359296 | tf_op jit(solution)/shard_map/reduce_scatter | solution.py:316
  19.8 26.5 %collective-permute-start.1 = (bf16[2,8,128,128]{3,2,1,0:T(8,128)(2,1)S(1)}, bf16[2,8,128,128]{3,2,1,0:T(8,128)(2,1)S(1)}, u32[]{:S(2)}, u32[]{:S(2)}) collective-permute-start(bf16[2,8,128,128]{3,2,1,0:T(8,128)(2,1)S(1)} %pad_maximum_fusion.refs_0_.refs_1_), channel_id=1, source_target_pairs={{0,32},{8,40},{16,48},{24,56},{32,64},{40,72},{48,80},{56,88},{64,... | collective-permute-start | bytes 1572872 | tf_op jit(solution)/shard_map/ppermute | solution.py:282
  21.2 26.8 %collective-permute-start.2 = (bf16[2,8,128,128]{3,2,1,0:T(8,128)(2,1)S(1)}, bf16[2,8,128,128]{3,2,1,0:T(8,128)(2,1)S(1)}, u32[]{:S(2)}, u32[]{:S(2)}) collective-permute-start(bf16[2,8,128,128]{3,2,1,0:T(8,128)(2,1)S(1)} %pad_maximum_fusion.refs_0_.refs_1_), channel_id=1, source_target_pairs={{0,64},{8,72},{16,80},{24,88},{32,96},{40,104},{48,112},{56,120},{... | collective-permute-start | bytes 1572872 | tf_op jit(solution)/shard_map/ppermute | solution.py:282
  25.0 31.9 %collective-permute-start.9 = (bf16[2,8,128,128]{3,2,1,0:T(8,128)(2,1)S(1)}, bf16[2,8,128,128]{3,2,1,0:T(8,128)(2,1)S(1)}, u32[]{:S(2)}, u32[]{:S(2)}) collective-permute-start(bf16[2,8,128,128]{3,2,1,0:T(8,128)(2,1)S(1)} %pad_maximum_fusion.2.refs_1_.refs_0_), channel_id=1, source_target_pairs={{0,32},{8,40},{16,48},{24,56},{32,64},{40,72},{48,80},{56,88},{64,... | collective-permute-start | bytes 1572872 | tf_op jit(solution)/shard_map/ppermute | solution.py:282
  25.7 41.6 %collective-permute-start.10 = (bf16[2,8,128,128]{3,2,1,0:T(8,128)(2,1)S(1)}, bf16[2,8,128,128]{3,2,1,0:T(8,128)(2,1)S(1)}, u32[]{:S(2)}, u32[]{:S(2)}) collective-permute-start(bf16[2,8,128,128]{3,2,1,0:T(8,128)(2,1)S(1)} %pad_maximum_fusion.2.refs_1_.refs_0_), channel_id=1, source_target_pairs={{0,64},{8,72},{16,80},{24,88},{32,96},{40,104},{48,112},{56,120},{... | collective-permute-start | bytes 1572872 | tf_op jit(solution)/shard_map/ppermute | solution.py:282
  28.4 38.9 %collective-permute-start.11 = (bf16[2,8,128,128]{3,2,1,0:T(8,128)(2,1)S(1)}, bf16[2,8,128,128]{3,2,1,0:T(8,128)(2,1)}, u32[]{:S(2)}, u32[]{:S(2)}) collective-permute-start(bf16[2,8,128,128]{3,2,1,0:T(8,128)(2,1)S(1)} %pad_maximum_fusion.2.refs_1_.refs_0_), channel_id=1, source_target_pairs={{0,96},{8,104},{16,112},{24,120},{32,0},{40,8},{48,16},{56,24},{64... | collective-permute-start | bytes 1572872 | tf_op jit(solution)/shard_map/ppermute | solution.py:282
  46.4 21.5 %collective-permute-start.3 = (bf16[2,8,128,128]{3,2,1,0:T(8,128)(2,1)S(1)}, bf16[2,8,128,128]{3,2,1,0:T(8,128)(2,1)}, u32[]{:S(2)}, u32[]{:S(2)}) collective-permute-start(bf16[2,8,128,128]{3,2,1,0:T(8,128)(2,1)S(1)} %pad_maximum_fusion.refs_0_.refs_1_), channel_id=1, source_target_pairs={{0,96},{8,104},{16,112},{24,120},{32,0},{40,8},{48,16},{56,24},{64... | collective-permute-start | bytes 1572872 | tf_op jit(solution)/shard_map/ppermute | solution.py:282
  48.1 19.9 %collective-permute-start.12 = (bf16[2,8,128,128]{3,2,1,0:T(8,128)(2,1)S(1)}, bf16[2,8,128,128]{3,2,1,0:T(8,128)(2,1)S(1)}, u32[]{:S(2)}, u32[]{:S(2)}) collective-permute-start(bf16[2,8,128,128]{3,2,1,0:T(8,128)(2,1)S(1)} %pad_maximum_fusion.2.refs_1_.refs_0_), channel_id=1, source_target_pairs={{0,8},{8,0},{16,24},{24,16},{32,40},{40,32},{48,56},{56,48},{64,72... | collective-permute-start | bytes 1572872 | tf_op jit(solution)/shard_map/ppermute | solution.py:274
  67.8 16.2 %collective-permute-start.4 = (bf16[2,8,128,128]{3,2,1,0:T(8,128)(2,1)S(1)}, bf16[2,8,128,128]{3,2,1,0:T(8,128)(2,1)}, u32[]{:S(2)}, u32[]{:S(2)}) collective-permute-start(bf16[2,8,128,128]{3,2,1,0:T(8,128)(2,1)S(1)} %pad_maximum_fusion.refs_0_.refs_1_), channel_id=1, source_target_pairs={{0,8},{8,0},{16,24},{24,16},{32,40},{40,32},{48,56},{56,48},{64,72... | collective-permute-start | bytes 1572872 | tf_op jit(solution)/shard_map/ppermute | solution.py:274
  67.9 16.2 %collective-permute-start.5 = (bf16[2,8,128,128]{3,2,1,0:T(8,128)(2,1)S(1)}, bf16[2,8,128,128]{3,2,1,0:T(8,128)(2,1)}, u32[]{:S(2)}, u32[]{:S(2)}) collective-permute-start(bf16[2,8,128,128]{3,2,1,0:T(8,128)(2,1)S(1)} %collective-permute-done.1.refs_1_.refs_2_), channel_id=1, source_target_pairs={{0,8},{8,0},{16,24},{24,16},{32,40},{40,32},{48,56},{56,48},{64,72... | collective-permute-start | bytes 1572872 | tf_op jit(solution)/shard_map/ppermute | solution.py:274
  68.4 15.7 %collective-permute-start.6 = (bf16[2,8,128,128]{3,2,1,0:T(8,128)(2,1)S(1)}, bf16[2,8,128,128]{3,2,1,0:T(8,128)(2,1)}, u32[]{:S(2)}, u32[]{:S(2)}) collective-permute-start(bf16[2,8,128,128]{3,2,1,0:T(8,128)(2,1)S(1)} %collective-permute-done.2.refs_2_.refs_3_), channel_id=1, source_target_pairs={{0,8},{8,0},{16,24},{24,16},{32,40},{40,32},{48,56},{56,48},{64,72... | collective-permute-start | bytes 1572872 | tf_op jit(solution)/shard_map/ppermute | solution.py:274
  69.2 14.9 %collective-permute-start.7 = (bf16[2,8,128,128]{3,2,1,0:T(8,128)(2,1)}, bf16[2,8,128,128]{3,2,1,0:T(8,128)(2,1)}, u32[]{:S(2)}, u32[]{:S(2)}) collective-permute-start(bf16[2,8,128,128]{3,2,1,0:T(8,128)(2,1)} %collective-permute-done.3.refs_3_.refs_4_), channel_id=1, source_target_pairs={{0,8},{8,0},{16,24},{24,16},{32,40},{40,32},{48,56},{56,48},{64,72... | collective-permute-start | bytes 1572872 | tf_op jit(solution)/shard_map/ppermute | solution.py:274
  93.4 113.2 %reduce-scatter.5.cloned.1.call-start = ((), (), s32[]{:S(2)}) async-start(), calls=%async_computation.3 | async-start | bytes 2359296 | tf_op jit(solution)/shard_map/reduce_scatter | solution.py:316
  120.5 13.1 %collective-permute-start.21 = (bf16[2,8,128,128]{3,2,1,0:T(8,128)(2,1)S(1)}, bf16[2,8,128,128]{3,2,1,0:T(8,128)(2,1)S(1)}, u32[]{:S(2)}, u32[]{:S(2)}) collective-permute-start(bf16[2,8,128,128]{3,2,1,0:T(8,128)(2,1)S(1)} %get-tuple-element.24), channel_id=1, source_target_pairs={{0,8},{8,0},{16,24},{24,16},{32,40},{40,32},{48,56},{56,48},{64,72... | collective-permute-start | bytes 1572872 | tf_op jit(solution)/shard_map/ppermute | solution.py:274
  134.3 24.7 %collective-permute-start.22 = (bf16[2,8,128,128]{3,2,1,0:T(8,128)(2,1)S(1)}, bf16[2,8,128,128]{3,2,1,0:T(8,128)(2,1)S(1)}, u32[]{:S(2)}, u32[]{:S(2)}) collective-permute-start(bf16[2,8,128,128]{3,2,1,0:T(8,128)(2,1)S(1)} %get-tuple-element.28), channel_id=1, source_target_pairs={{0,96},{8,104},{16,112},{24,120},{32,0},{40,8},{48,16},{56,24},{64... | collective-permute-start | bytes 1572872 | tf_op jit(solution)/shard_map/ppermute | solution.py:282
  135.9 24.9 %collective-permute-start.20 = (bf16[2,8,128,128]{3,2,1,0:T(8,128)(2,1)S(1)}, bf16[2,8,128,128]{3,2,1,0:T(8,128)(2,1)S(1)}, u32[]{:S(2)}, u32[]{:S(2)}) collective-permute-start(bf16[2,8,128,128]{3,2,1,0:T(8,128)(2,1)S(1)} %get-tuple-element.29), channel_id=1, source_target_pairs={{0,64},{8,72},{16,80},{24,88},{32,96},{40,104},{48,112},{56,120},{... | collective-permute-start | bytes 1572872 | tf_op jit(solution)/shard_map/ppermute | solution.py:282
  137.8 26.1 %collective-permute-start.18 = (bf16[2,8,128,128]{3,2,1,0:T(8,128)(2,1)S(1)}, bf16[2,8,128,128]{3,2,1,0:T(8,128)(2,1)S(1)}, u32[]{:S(2)}, u32[]{:S(2)}) collective-permute-start(bf16[2,8,128,128]{3,2,1,0:T(8,128)(2,1)S(1)} %get-tuple-element.27), channel_id=1, source_target_pairs={{0,32},{8,40},{16,48},{24,56},{32,64},{40,72},{48,80},{56,88},{64,... | collective-permute-start | bytes 1572872 | tf_op jit(solution)/shard_map/ppermute | solution.py:282
  137.8 27.4 %collective-permute-start.25 = (bf16[2,8,128,128]{3,2,1,0:T(8,128)(2,1)S(1)}, bf16[2,8,128,128]{3,2,1,0:T(8,128)(2,1)S(1)}, u32[]{:S(2)}, u32[]{:S(2)}) collective-permute-start(bf16[2,8,128,128]{3,2,1,0:T(8,128)(2,1)S(1)} %get-tuple-element.16), channel_id=1, source_target_pairs={{0,8},{8,0},{16,24},{24,16},{32,40},{40,32},{48,56},{56,48},{64,72... | collective-permute-start | bytes 1572872 | tf_op jit(solution)/shard_map/ppermute | solution.py:274
  138.7 32.9 %collective-permute-start.31 = (bf16[2,8,128,128]{3,2,1,0:T(8,128)(2,1)S(1)}, bf16[2,8,128,128]{3,2,1,0:T(8,128)(2,1)S(1)}, u32[]{:S(2)}, u32[]{:S(2)}) collective-permute-start(bf16[2,8,128,128]{3,2,1,0:T(8,128)(2,1)S(1)} %get-tuple-element.21), channel_id=1, source_target_pairs={{0,96},{8,104},{16,112},{24,120},{32,0},{40,8},{48,16},{56,24},{64... | collective-permute-start | bytes 1572872 | tf_op jit(solution)/shard_map/ppermute | solution.py:282
  158.9 16.4 %collective-permute-start.29 = (bf16[2,8,128,128]{3,2,1,0:T(8,128)(2,1)S(1)}, bf16[2,8,128,128]{3,2,1,0:T(8,128)(2,1)S(1)}, u32[]{:S(2)}, u32[]{:S(2)}) collective-permute-start(bf16[2,8,128,128]{3,2,1,0:T(8,128)(2,1)S(1)} %get-tuple-element.22), channel_id=1, source_target_pairs={{0,64},{8,72},{16,80},{24,88},{32,96},{40,104},{48,112},{56,120},{... | collective-permute-start | bytes 1572872 | tf_op jit(solution)/shard_map/ppermute | solution.py:282
  160.8 24.0 %collective-permute-start.27 = (bf16[2,8,128,128]{3,2,1,0:T(8,128)(2,1)S(1)}, bf16[2,8,128,128]{3,2,1,0:T(8,128)(2,1)S(1)}, u32[]{:S(2)}, u32[]{:S(2)}) collective-permute-start(bf16[2,8,128,128]{3,2,1,0:T(8,128)(2,1)S(1)} %get-tuple-element.20), channel_id=1, source_target_pairs={{0,32},{8,40},{16,48},{24,56},{32,64},{40,72},{48,80},{56,88},{64,... | collective-permute-start | bytes 1572872 | tf_op jit(solution)/shard_map/ppermute | solution.py:282
  164.4 21.4 %collective-permute-start.23 = (bf16[8,128,128]{2,1,0:T(8,128)(2,1)S(1)}, bf16[8,128,128]{2,1,0:T(8,128)(2,1)S(1)}, u32[]{:S(2)}, u32[]{:S(2)}) collective-permute-start(bf16[8,128,128]{2,1,0:T(8,128)(2,1)S(1)} %fusion.16), channel_id=1, source_target_pairs={{0,16},{8,24},{16,0},{24,8},{32,48},{40,56},{48,32},{56,40},{64,80... | collective-permute-start | bytes 786440 | tf_op jit(solution)/shard_map/ppermute | solution.py:278
  185.8 15.4 %collective-permute-start.24 = (bf16[8,128,128]{2,1,0:T(8,128)(2,1)S(1)}, bf16[8,128,128]{2,1,0:T(8,128)(2,1)S(1)}, u32[]{:S(2)}, u32[]{:S(2)}) collective-permute-start(bf16[8,128,128]{2,1,0:T(8,128)(2,1)S(1)} %fusion.15), channel_id=1, source_target_pairs={{0,128},{128,0},{1,129},{129,1},{2,130},{130,2},{3,131},{131,3},{4... | collective-permute-start | bytes 786440 | tf_op jit(solution)/shard_map/ppermute | solution.py:286
  (24 other events, 344.9 us)
Sparse Core Ops, SparseCore 0:
  9.8 57.6 all-gather.2
  93.5 43.7 reduce-scatter.2
  140.5 40.6 reduce-scatter.4
